TPU v7x, 32 devices: a whole 2x2x4 slice. The times are simulated.
32 devices in a mesh: pipe: 1, expert: 32 (over z, y, x, core).
Axes of the slice: x: 2, y: 2, z: 4, core: 2. Of those that a mesh axis runs over, the one named last changes fastest.
Arguments:
- inputs: bfloat16 [1, 2, 2048, 2048], P('pipe', None, 'expert'), may hold values from -6 to 6
- grads_out: bfloat16 [1, 2, 2048, 2048], P('pipe', None, 'expert'), may hold values from -6 to 6
- expert_ids: int32 [1, 2, 2048, 6], P('pipe', None, 'expert'), may hold values from 0 to 31, all different within a row; in each aligned block of 64 rows (0 to 63, 64 to 127, ..., all dimensions but the last counted through in order) at most 32 rows name the same one
- gate_values: float32 [1, 2, 2048, 6], P('pipe', None, 'expert'), may hold values from 0.1 to 0.5
- w_gate: bfloat16 [1, 32, 2048, 768], P('pipe', 'expert'), may hold values from -0.125 to 0.125
- w_up: bfloat16 [1, 32, 2048, 768], P('pipe', 'expert'), may hold values from -0.125 to 0.125
- w_down: bfloat16 [1, 32, 768, 2048], P('pipe', 'expert'), may hold values from -0.21875 to 0.21875
Outputs:
- received: bfloat16 [1, 2, 2048, 2048], P('pipe', None, 'expert')
- gate_grad: float32 [1, 2, 2048, 6], P('pipe', None, 'expert')
Inputs may be any that keep to these rules, and one draw needn't show every extreme that they name: `expert_ids`: each row names 6 different experts. Within the 64 rows of one device for one section and micro-batch, no expert is named by more than 32 rows, a bound that some expert reaches in some of these blocks.
All inputs are finite; a program needn't handle non-finite values.
Results may differ from a plain program's by a relative error of at most 0.0041.
Values may be sent and summed in bfloat16 or wider, within the bound.
A program may use at most 128 MiB of HBM per device.

v0:
```python
import jax
import jax.numpy as jnp
from jax import lax
from jax.sharding import PartitionSpec as P


def shortened(array):
    return jax.tree.map(lambda a: a.astype(jnp.bfloat16) if a.dtype == jnp.float32 else a, array)


def from_behind(value, axis, steps):
    count = lax.axis_size(axis)
    pairs = [(source, (source + steps) % count) for source in range(count)]
    return lax.ppermute(value, axis, pairs)


def expert_rows(x_rows, grad_rows, gate_weight, up_weight, down_weight):
    gate_pre = jnp.dot(x_rows, gate_weight, preferred_element_type=jnp.float32)
    up_pre = jnp.dot(x_rows, up_weight, preferred_element_type=jnp.float32)
    back_grad = lax.dot_general(
        grad_rows, down_weight, (((1,), (1,)), ((), ())), preferred_element_type=jnp.float32
    )
    logistic = jax.nn.sigmoid(gate_pre)
    swish = gate_pre * logistic
    score = jnp.sum(back_grad * swish * up_pre, axis=1).astype(jnp.bfloat16)
    d_gate = (back_grad * up_pre * logistic * (1.0 + gate_pre * (1.0 - logistic))).astype(
        jnp.bfloat16
    )
    d_up = (back_grad * swish).astype(jnp.bfloat16)
    pair_grad = lax.dot_general(
        d_gate, gate_weight, (((1,), (1,)), ((), ())), preferred_element_type=jnp.float32
    )
    pair_grad = pair_grad + lax.dot_general(
        d_up, up_weight, (((1,), (1,)), ((), ())), preferred_element_type=jnp.float32
    )
    return (pair_grad.astype(jnp.bfloat16), score)


def slot_table(ids_group, experts, capacity):
    groups, rows, picks = ids_group.shape
    flat_ids = ids_group.reshape(groups, rows * picks)
    onehot = (flat_ids[:, :, None] == jnp.arange(experts, dtype=jnp.int32)[None, None, :]).astype(
        jnp.int32
    )
    earlier = jnp.cumsum(onehot, axis=1) - onehot
    position = jnp.sum(earlier * onehot, axis=2)
    counts = jnp.sum(onehot, axis=1)
    group_index = jnp.arange(groups, dtype=jnp.int32)[:, None]
    target = flat_ids * (groups * capacity) + group_index * capacity + position
    return (target.reshape(-1), counts)


def expert_pass(x_group, grad_group, ids_group, seen, weights, send, bring_back, capacity):
    experts = seen.shape[0]
    groups, rows, width = x_group.shape
    picks = ids_group.shape[2]
    target, unused_counts = slot_table(ids_group, experts, capacity)
    total = experts * groups * capacity
    token_of = jnp.arange(groups * rows * picks, dtype=jnp.int32) // picks
    x_flat = x_group.reshape(groups * rows, width)
    grad_flat = grad_group.reshape(groups * rows, width)
    send_x = jnp.zeros((total, width), jnp.bfloat16).at[target].set(x_flat[token_of])
    send_grad = jnp.zeros((total, width), jnp.bfloat16).at[target].set(grad_flat[token_of])
    got_x, got_grad = send(
        (
            send_x.reshape(experts, groups * capacity, width),
            send_grad.reshape(experts, groups * capacity, width),
        )
    )
    slot = jnp.arange(groups * capacity, dtype=jnp.int32)
    limit = seen[:, slot // capacity]
    live = ((slot % capacity)[None, :] < limit).reshape(-1)
    block = min(256, total)
    padded = (total + block - 1) // block * block
    order = jnp.cumsum(live.astype(jnp.int32)) - 1
    used = jnp.sum(live.astype(jnp.int32))
    place = jnp.where(live, order, padded)
    pack_x = (
        jnp.zeros((padded, width), jnp.bfloat16)
        .at[place]
        .set(got_x.reshape(total, width), mode="drop")
    )
    pack_grad = (
        jnp.zeros((padded, width), jnp.bfloat16)
        .at[place]
        .set(got_grad.reshape(total, width), mode="drop")
    )
    gate_weight, up_weight, down_weight = weights

    def one_block(index, carry):
        block_grads, block_scores = carry
        start = index * block
        grad_rows, score_rows = expert_rows(
            lax.dynamic_slice_in_dim(pack_x, start, block, 0),
            lax.dynamic_slice_in_dim(pack_grad, start, block, 0),
            gate_weight,
            up_weight,
            down_weight,
        )
        return (
            lax.dynamic_update_slice_in_dim(block_grads, grad_rows, start, 0),
            lax.dynamic_update_slice_in_dim(block_scores, score_rows, start, 0),
        )

    empty = (jnp.zeros((padded, width), jnp.bfloat16), jnp.zeros((padded,), jnp.bfloat16))
    block_grads, block_scores = lax.fori_loop(0, (used + block - 1) // block, one_block, empty)
    source = jnp.minimum(place, padded - 1)
    out_rows = jnp.where(live[:, None], block_grads[source], jnp.zeros((), jnp.bfloat16))
    out_scores = jnp.where(live, block_scores[source], jnp.zeros((), jnp.bfloat16))
    ret_rows, ret_scores = bring_back(
        (
            out_rows.reshape(experts, groups * capacity, width),
            out_scores.reshape(experts, groups * capacity),
        )
    )
    pair_grad = ret_rows.reshape(total, width)[target].reshape(groups, rows, picks, width)
    pair_score = ret_scores.reshape(total)[target].reshape(groups, rows, picks)
    return (pair_grad, pair_score)


def on_device(inputs, grads_out, expert_ids, gate_values, w_gate, w_up, w_down):
    experts = lax.axis_size("expert")
    self_index = lax.axis_index("expert")
    x_all = inputs[0]
    grad_all = grads_out[0]
    ids_all = expert_ids[0]
    gates_all = gate_values[0]
    micro_count, rows, width = x_all.shape
    picks = ids_all.shape[2]
    capacity = min(rows, 8 * rows * picks // (3 * experts))
    unused_target, local_counts = slot_table(ids_all, experts, capacity)
    table = lax.all_gather(local_counts[None], "expert", axis=0, tiled=True)
    seen = jnp.take(table, self_index, axis=2)
    weights = (w_gate[0, 0], w_up[0, 0], w_down[0, 0])
    delivered = []
    scores = []

    def send_each(pair):
        return jax.tree.map(
            lambda part, own: part.astype(own.dtype),
            lax.all_to_all(shortened(pair), "expert", split_axis=0, concat_axis=0, tiled=True),
            pair,
        )

    def back_each(pair):
        return jax.tree.map(
            lambda part, own: part.astype(own.dtype),
            lax.all_to_all(shortened(pair), "expert", split_axis=0, concat_axis=0, tiled=True),
            pair,
        )

    for micro in range(micro_count):
        pair_grad, pair_score = expert_pass(
            x_all[micro : micro + 1],
            grad_all[micro : micro + 1],
            ids_all[micro : micro + 1],
            seen[:, micro : micro + 1],
            weights,
            send_each,
            back_each,
            capacity,
        )
        gates_part = gates_all[micro : micro + 1]
        combined = grad_all[micro : micro + 1].astype(jnp.float32) + jnp.sum(
            gates_part[..., None] * pair_grad.astype(jnp.float32), axis=2
        )
        moved = combined.astype(jnp.bfloat16)[None]
        score_part = pair_score.astype(jnp.float32)
        delivered.append(moved)
        scores.append(score_part)
    received = jnp.concatenate(delivered, axis=1)
    received = from_behind(received, "pipe", -1)
    gate_grad = jnp.concatenate(scores, axis=0)[None]
    return (received, gate_grad)


def solution(mesh):
    placed = (
        P("pipe", None, "expert", None),
        P("pipe", None, "expert", None),
        P("pipe", None, "expert", None),
        P("pipe", None, "expert", None),
        P("pipe", "expert", None, None),
        P("pipe", "expert", None, None),
        P("pipe", "expert", None, None),
    )
    return jax.shard_map(
        on_device,
        mesh=mesh,
        in_specs=placed,
        out_specs=(P("pipe", None, "expert", None), P("pipe", None, "expert", None)),
        check_vma=False,
    )
```

profile of v0, /device:TPU:0, one launch (start us, length us, event | category | flops | bytes accessed | tf_op | source)
XLA Modules:
  0.0 720.5 jit_solution(1070911775478979147)
XLA Ops:
  4.4 10.5 %scatter_custom_fusion = bf16[1024,2048]{1,0:T(8,128)(2,1)} fusion(s32[384]{0:T(512)S(1)} %fusion.59, bf16[]{:T(256)} %constant.139.clone.1, bf16[64,2048]{1,0:T(8,128)(2,1)S(1)} %get-tuple-element.165, s32[1024]{0:T(1024)S(1)} %pad_clamp_fusion.2), kind=kCustom, calls=%fused_computation.78 | custom fusion | bytes 4194306 | tf_op jit(solution)/shard_map/scatter | solution.py:63
  14.9 7.6 %all-to-all-start = ((bf16[32,32,2048]{2,1,0:T(8,128)(2,1)}), bf16[32,32,2048]{2,1,0:T(8,128)(2,1)}, u32[]{:S(2)}, u32[]{:S(2)}) async-start(bf16[32,32,2048]{2,1,0:T(8,128)(2,1)} %bitcast.143), calls=%async_computation | async-start | bytes 8388608 | tf_op jit(solution)/shard_map/all_to_all | solution.py:141
  22.6 10.5 %scatter_custom_fusion.2 = bf16[1024,2048]{1,0:T(8,128)(2,1)} fusion(s32[384]{0:T(512)S(1)} %fusion.59, bf16[]{:T(256)} %constant.139.clone.1, bf16[64,2048]{1,0:T(8,128)(2,1)S(1)} %get-tuple-element.163, s32[1024]{0:T(1024)S(1)} %pad_clamp_fusion.2), kind=kCustom, calls=%fused_computation.74 | custom fusion | bytes 4194306 | tf_op jit(solution)/shard_map/scatter | solution.py:62
  33.1 83.4 %all-to-all-done = bf16[32,32,2048]{2,1,0:T(8,128)(2,1)} async-done(((bf16[32,32,2048]{2,1,0:T(8,128)(2,1)}), bf16[32,32,2048]{2,1,0:T(8,128)(2,1)}, u32[]{:S(2)}, u32[]{:S(2)}) %all-to-all-start) | async-done | bytes 4194336 | tf_op jit(solution)/shard_map/all_to_all | solution.py:141
  122.6 10.4 %scatter_custom_fusion.4 = bf16[1024,2048]{1,0:T(8,128)(2,1)} fusion(s32[384]{0:T(512)S(1)} %fusion.61, bf16[]{:T(256)} %constant.139.clone.1, bf16[64,2048]{1,0:T(8,128)(2,1)S(1)} %get-tuple-element.166, s32[1024]{0:T(1024)S(1)} %pad_clamp_fusion.2), kind=kCustom, calls=%fused_computation.70 | custom fusion | bytes 4194306 | tf_op jit(solution)/shard_map/scatter | solution.py:63
  133.1 81.6 %all-to-all-done.1 = bf16[32,32,2048]{2,1,0:T(8,128)(2,1)} async-done(((bf16[32,32,2048]{2,1,0:T(8,128)(2,1)}), bf16[32,32,2048]{2,1,0:T(8,128)(2,1)}, u32[]{:S(2)}, u32[]{:S(2)}) %all-to-all-start.1) | async-done | bytes 4194336 | tf_op jit(solution)/shard_map/all_to_all | solution.py:141
  219.1 103.4 %all-gather.1 = s32[32,2,32]{2,1,0:T(2,128)S(1)} all-gather(s32[1,2,32]{2,1,0:T(2,128)S(1)} %bitcast.153), channel_id=2, replica_groups=mesh['pipe'=1,'expert'=32] {'expert'}, dimensions={0}, use_global_device_ids=true | all-gather | bytes 8448 | tf_op jit(solution)/shard_map/all_gather | solution.py:132
  326.3 10.6 %scatter_custom_fusion.6 = bf16[1024,2048]{1,0:T(8,128)(2,1)} fusion(s32[384]{0:T(512)S(1)} %fusion.61, bf16[]{:T(256)} %constant.139.clone.1, bf16[64,2048]{1,0:T(8,128)(2,1)S(1)} %get-tuple-element.164, s32[1024]{0:T(1024)S(1)} %pad_clamp_fusion.2), kind=kCustom, calls=%fused_computation.66 | custom fusion | bytes 4194306 | tf_op jit(solution)/shard_map/scatter | solution.py:62
  337.4 10.1 %scatter_custom_fusion.1 = bf16[1024,2048]{1,0:T(8,128)(2,1)} fusion(s32[1024]{0:T(1024)S(1)} %bitcast.156, bf16[1024,2048]{1,0:T(8,128)(2,1)} %bitcast.11, bf16[]{:T(256)} %constant.139.clone.1), kind=kCustom, calls=%fused_computation.76 | custom fusion | bytes 4194816 | tf_op jit(solution)/shard_map/scatter | solution.py:86
  347.4 10.1 %scatter_custom_fusion.3 = bf16[1024,2048]{1,0:T(8,128)(2,1)} fusion(s32[1024]{0:T(1024)S(1)} %bitcast.157, bf16[1024,2048]{1,0:T(8,128)(2,1)} %bitcast.15, bf16[]{:T(256)} %constant.139.clone.1), kind=kCustom, calls=%fused_computation.72 | custom fusion | bytes 4194816 | tf_op jit(solution)/shard_map/scatter | solution.py:81
  357.5 17.7 %all-to-all-start.4 = ((bf16[32,32,2048]{2,1,0:T(8,128)(2,1)}), bf16[32,32,2048]{2,1,0:T(8,128)(2,1)}, u32[]{:S(2)}, u32[]{:S(2)}) async-start(bf16[32,32,2048]{2,1,0:T(8,128)(2,1)} %bitcast.141), calls=%async_computation.4 | async-start | bytes 8388608 | tf_op jit(solution)/shard_map/all_to_all | solution.py:141
  377.7 23.3 %while.25 = (s32[]{:T(128)}, bf16[1024,2048]{1,0:T(8,128)(2,1)}, bf16[1024]{0:T(1024)(128)(2,1)S(1)}, s32[]{:T(128)}, bf16[1024,2048]{1,0:T(8,128)(2,1)}, /*inde...) while((s32[]{:T(128)}, bf16[1024,2048]{1,0:T(8,128)(2,1)}, ...), condition=%wide.region_13.14_spmd, body=%wide.region_11.13_spmd.sunk | while | flops 4032102144 | bytes 69732112 | solution.py:106
  401.0 11.6 %gather_fusion = bf16[1024,2048]{1,0:T(8,128)(2,1)} fusion(bf16[1024,2048]{1,0:T(8,128)(2,1)} %get-tuple-element.100, s32[1024]{0:T(1024)S(1)} %broadcast_clamp_fusion.1), kind=kCustom, calls=%fused_computation.2 | custom fusion | bytes 8392704 | tf_op jit(solution)/shard_map/gather | solution.py:108
  412.6 10.1 %scatter_custom_fusion.5 = bf16[1024,2048]{1,0:T(8,128)(2,1)} fusion(s32[1024]{0:T(1024)S(1)} %bitcast.154, bf16[1024,2048]{1,0:T(8,128)(2,1)} %bitcast.31, bf16[]{:T(256)} %constant.139.clone.1), kind=kCustom, calls=%fused_computation.68 | custom fusion | bytes 4194816 | tf_op jit(solution)/shard_map/scatter | solution.py:86
  427.1 42.0 %all-to-all-done.4 = bf16[32,32,2048]{2,1,0:T(8,128)(2,1)} async-done(((bf16[32,32,2048]{2,1,0:T(8,128)(2,1)}), bf16[32,32,2048]{2,1,0:T(8,128)(2,1)}, u32[]{:S(2)}, u32[]{:S(2)}) %all-to-all-start.4) | async-done | bytes 4194336 | tf_op jit(solution)/shard_map/all_to_all | solution.py:141
  473.6 10.0 %scatter_custom_fusion.7 = bf16[1024,2048]{1,0:T(8,128)(2,1)} fusion(s32[1024]{0:T(1024)S(1)} %bitcast.155, bf16[1024,2048]{1,0:T(8,128)(2,1)} %bitcast.34, bf16[]{:T(256)} %constant.139.clone.1), kind=kCustom, calls=%fused_computation.64 | custom fusion | bytes 4194816 | tf_op jit(solution)/shard_map/scatter | solution.py:81
  486.2 23.1 %while.26 = (s32[]{:T(128)}, bf16[1024,2048]{1,0:T(8,128)(2,1)}, bf16[1024]{0:T(1024)(128)(2,1)S(1)}, s32[]{:T(128)}, bf16[1024,2048]{1,0:T(8,128)(2,1)}, /*inde...) while((s32[]{:T(128)}, bf16[1024,2048]{1,0:T(8,128)(2,1)}, ...), condition=%wide.region_27.28_spmd, body=%wide.region_25.27_spmd.sunk | while | flops 4032102144 | bytes 69732112 | solution.py:106
  509.2 11.5 %gather_fusion.2 = bf16[1024,2048]{1,0:T(8,128)(2,1)} fusion(bf16[1024,2048]{1,0:T(8,128)(2,1)} %get-tuple-element.101, s32[1024]{0:T(1024)S(1)} %broadcast_clamp_fusion), kind=kCustom, calls=%fused_computation.6 | custom fusion | bytes 8392704 | tf_op jit(solution)/shard_map/gather | solution.py:108
  525.3 42.2 %all-to-all-done.2 = bf16[32,32,2048]{2,1,0:T(8,128)(2,1)} async-done(((bf16[32,32,2048]{2,1,0:T(8,128)(2,1)}), bf16[32,32,2048]{2,1,0:T(8,128)(2,1)}, u32[]{:S(2)}, u32[]{:S(2)}) %all-to-all-start.2) | async-done | bytes 4194336 | tf_op jit(solution)/shard_map/all_to_all | solution.py:148
  571.9 7.1 gather_fusion.1
  581.2 84.3 %all-to-all-done.5 = bf16[32,32,2048]{2,1,0:T(8,128)(2,1)} async-done(((bf16[32,32,2048]{2,1,0:T(8,128)(2,1)}), bf16[32,32,2048]{2,1,0:T(8,128)(2,1)}, u32[]{:S(2)}, u32[]{:S(2)}) %all-to-all-start.5) | async-done | bytes 4194336 | tf_op jit(solution)/shard_map/all_to_all | solution.py:148
  665.5 7.1 gather_fusion.3
  680.4 6.8 gather_fusion.4
  687.3 6.8 gather_fusion.6
  (187 shorter events, 121.9 us)
Async XLA Ops:
  4.4 18.2 %copy-start.10 = (s32[384]{0:T(512)}, s32[384]{0:T(512)S(1)}, u32[]{:S(2)}) copy-start(s32[384]{0:T(512)S(1)} %fusion.59) | copy-start | bytes 4612
  14.9 7.6 %copy-start.2 = (bf16[1,2,64,2048]{3,2,1,0:T(8,128)(2,1)S(1)}, bf16[1,2,64,2048]{3,2,1,0:T(8,128)(2,1)}, u32[]{:S(2)}) copy-start(bf16[1,2,64,2048]{3,2,1,0:T(8,128)(2,1)} %param.11) | copy-start | bytes 1572868
  14.9 101.5 %all-to-all-start = ((bf16[32,32,2048]{2,1,0:T(8,128)(2,1)}), bf16[32,32,2048]{2,1,0:T(8,128)(2,1)}, u32[]{:S(2)}, u32[]{:S(2)}) async-start(bf16[32,32,2048]{2,1,0:T(8,128)(2,1)} %bitcast.143), calls=%async_computation | async-start | bytes 8388608 | tf_op jit(solution)/shard_map/all_to_all | solution.py:141
  116.5 98.2 %all-to-all-start.1 = ((bf16[32,32,2048]{2,1,0:T(8,128)(2,1)}), bf16[32,32,2048]{2,1,0:T(8,128)(2,1)}, u32[]{:S(2)}, u32[]{:S(2)}) async-start(bf16[32,32,2048]{2,1,0:T(8,128)(2,1)} %bitcast.142), calls=%async_computation.1 | async-start | bytes 8388608 | tf_op jit(solution)/shard_map/all_to_all | solution.py:141
  214.6 4.1 copy-start.3
  214.6 142.9 %all-to-all-start.3 = ((bf16[32,32,2048]{2,1,0:T(8,128)(2,1)}), bf16[32,32,2048]{2,1,0:T(8,128)(2,1)}, u32[]{:S(2)}, u32[]{:S(2)}) async-start(bf16[32,32,2048]{2,1,0:T(8,128)(2,1)} %bitcast.140), calls=%async_computation.3 | async-start | bytes 8388608 | tf_op jit(solution)/shard_map/all_to_all | solution.py:141
  357.5 111.6 %all-to-all-start.4 = ((bf16[32,32,2048]{2,1,0:T(8,128)(2,1)}), bf16[32,32,2048]{2,1,0:T(8,128)(2,1)}, u32[]{:S(2)}, u32[]{:S(2)}) async-start(bf16[32,32,2048]{2,1,0:T(8,128)(2,1)} %bitcast.141), calls=%async_computation.4 | async-start | bytes 8388608 | tf_op jit(solution)/shard_map/all_to_all | solution.py:141
  377.9 3.4 copy-start.13
  378.0 5.6 copy-start.15
  389.5 5.6 copy-start.15
  469.1 98.4 %all-to-all-start.2 = ((bf16[32,32,2048]{2,1,0:T(8,128)(2,1)}), bf16[32,32,2048]{2,1,0:T(8,128)(2,1)}, u32[]{:S(2)}, u32[]{:S(2)}) async-start(bf16[32,32,2048]{2,1,0:T(8,128)(2,1)} %broadcast_select_fusion.1), calls=%async_computation.2 | async-start | bytes 8388608 | tf_op jit(solution)/shard_map/all_to_all | solution.py:148
  486.2 5.6 copy-start.16
  497.8 5.6 copy-start.16
  525.3 46.3 %copy-start.12 = (f32[1,2,64,6]{2,1,3,0:T(2,128)S(1)}, f32[1,2,64,6]{2,1,3,0:T(2,128)}, u32[]{:S(2)}) copy-start(f32[1,2,64,6]{2,1,3,0:T(2,128)} %param.14) | copy-start | bytes 9220
  525.3 46.5 %copy-start.11 = (s32[384]{0:T(512)S(1)}, s32[384]{0:T(512)}, u32[]{:S(2)}) copy-start(s32[384]{0:T(512)} %copy-done.10) | copy-start | bytes 4612
  567.6 97.9 %all-to-all-start.5 = ((bf16[32,32,2048]{2,1,0:T(8,128)(2,1)}), bf16[32,32,2048]{2,1,0:T(8,128)(2,1)}, u32[]{:S(2)}, u32[]{:S(2)}) async-start(bf16[32,32,2048]{2,1,0:T(8,128)(2,1)} %broadcast_select_fusion), calls=%async_computation.5 | async-start | bytes 8388608 | tf_op jit(solution)/shard_map/all_to_all | solution.py:148
  674.7 3.9 copy-start
  674.7 5.4 copy-start.1
  680.2 14.0 %copy-start.5 = (s32[32]{0:T(128)S(1)}, s32[32]{0:T(128)}, u32[]{:S(2)}) copy-start(s32[32]{0:T(128)} %copy-done.4) | copy-start | bytes 388
  680.2 14.0 %copy-start.7 = (s32[32]{0:T(128)S(1)}, s32[32]{0:T(128)}, u32[]{:S(2)}) copy-start(s32[32]{0:T(128)} %copy-done.6) | copy-start | bytes 388
  680.2 14.0 %copy-start.9 = (s32[32]{0:T(128)S(1)}, s32[32]{0:T(128)}, u32[]{:S(2)}) copy-start(s32[32]{0:T(128)} %copy-done.8) | copy-start | bytes 388
  680.4 39.1 %collective-permute-start = (bf16[1,2,64,2048]{3,2,1,0:T(8,128)(2,1)S(1)}, bf16[1,2,64,2048]{3,2,1,0:T(8,128)(2,1)S(1)}, u32[]{:S(2)}, u32[]{:S(2)}) collective-permute-start(bf16[1,2,64,2048]{3,2,1,0:T(8,128)(2,1)S(1)} %pad_maximum_fusion), channel_id=1, source_target_pairs={{0,0},{1,1},{2,2},{3,3},{4,4},{5,5},{6,6},{7,7},{8,8},{9,9},{10,10... | collective-permute-start | bytes 1572872 | tf_op jit(solution)/shard_map/ppermute | solution.py:14
  694.9 11.0 %all-to-all-start.7 = ((bf16[32,1,32]{2,1,0:T(2,128)(2,1)}), bf16[32,1,32]{2,1,0:T(2,128)(2,1)S(1)}, u32[]{:S(2)}, u32[]{:S(2)}) async-start(bf16[32,1,32]{2,1,0:T(2,128)(2,1)} %copy.105), calls=%async_computation.7 | async-start | bytes 32768 | tf_op jit(solution)/shard_map/all_to_all | solution.py:148
  706.0 9.7 %all-to-all-start.6 = ((bf16[32,1,32]{2,1,0:T(2,128)(2,1)}), bf16[32,1,32]{2,1,0:T(2,128)(2,1)S(1)}, u32[]{:S(2)}, u32[]{:S(2)}) async-start(bf16[32,1,32]{2,1,0:T(2,128)(2,1)} %copy.104), calls=%async_computation.6 | async-start | bytes 32768 | tf_op jit(solution)/shard_map/all_to_all | solution.py:148
  (10 other events, 27.3 us)
where the time goes:
time: 729 us; the launch traced here: 721 us
  waiting for transfers between devices  344 us (47%)
  local copies, waits for them, and re-layouts  157 us (22%)
  blocking collectives  103 us (14%)
  starting transfers between devices  48.7 us (7%)
  matrix products  45.1 us (6%)
  other arithmetic  19.2 us (3%)
    all_to_all x4, waiting for transfers between devices, send_each(): lax.all_to_all(shortened(pair), 'expert', split_axis=0, concat_axis=0, ti...  207 us
    all_to_all x4, waiting for transfers between devices, back_each(): lax.all_to_all(shortened(pair), 'expert', split_axis=0, concat_axis=0, ti...  137 us
    all_gather x1, blocking collectives, on_device(): table = lax.all_gather(local_counts[None], 'expert', axis=0, tiled=True)  103 us
    all_to_all x4, starting transfers between devices, send_each(): lax.all_to_all(shortened(pair), 'expert', split_axis=0, concat_axis=0, ti...  33.6 us
    gather x2, local copies, waits for them, and re-layouts, expert_pass(): block_grads[source]  23.1 us
    scatter x2, local copies, waits for them, and re-layouts, expert_pass(): jnp.zeros((total, width), jnp.bfloat16).at[target].set(x_flat[token_of])  21.1 us
    scatter x2, local copies, waits for them, and re-layouts, expert_pass(): jnp.zeros((total, width), jnp.bfloat16).at[target].set(grad_flat[token_of])  20.9 us
    scatter x2, local copies, waits for them, and re-layouts, expert_pass(): pack_grad = jnp.zeros((padded, width), jnp.bfloat16).at[place].set(got_gr...  20.1 us
  transfers between devices with their start and end apart: 9, of which 7 were waited for; matrix products, arithmetic and copies ran while one was open for 27% of the time, Pallas kernels for 0%

commit v1 on v0

--- a/solution.py
+++ b/solution.py
@@ -119,6 +119,29 @@
 
 
 def on_device(inputs, grads_out, expert_ids, gate_values, w_gate, w_up, w_down):
+
+    def frames_begin(z_in, shard_axis):
+        block_out, step_out, a_now = (
+            lax.axis_size(shard_axis),
+            lax.axis_index(shard_axis),
+            z_in.shape[0],
+        )
+        val2, w1 = (z_in, 1)
+        while w1 < block_out:
+            val2 = jnp.concatenate(
+                [
+                    val2,
+                    lax.ppermute(
+                        val2,
+                        shard_axis,
+                        tuple(((i0, (i0 - w1) % block_out) for i0 in range(block_out))),
+                    ),
+                ],
+                0,
+            )
+            w1 = 2 * w1
+        return jnp.roll(val2, step_out * a_now, 0)
+
     experts = lax.axis_size("expert")
     self_index = lax.axis_index("expert")
     x_all = inputs[0]
@@ -129,7 +152,7 @@
     picks = ids_all.shape[2]
     capacity = min(rows, 8 * rows * picks // (3 * experts))
     unused_target, local_counts = slot_table(ids_all, experts, capacity)
-    table = lax.all_gather(local_counts[None], "expert", axis=0, tiled=True)
+    table = frames_begin(local_counts[None], "expert")
     seen = jnp.take(table, self_index, axis=2)
     weights = (w_gate[0, 0], w_up[0, 0], w_down[0, 0])
     delivered = []

time: 729 us -> 698 us (0.957)
  blocking collectives: 103 us -> 0 us
  waiting for transfers between devices: 344 us -> 418 us
    all_gather x1 -> x0, blocking collectives: 103 us -> none  [on_device(): table = lax.all_gather(local_counts[None], 'expert', axis=0, tiled=True)]
    all_to_all x4, waiting for transfers between devices: 207 us -> 267 us  [send_each(): lax.all_to_all(shortened(pair), 'expert', split_axis=0, concat_axis=0, ti...]
    ppermute x0 -> x5, waiting for transfers between devices: none -> 13.7 us  [frames_begin(): lax.ppermute(val2, shard_axis, tuple(((i0, (i0 - w1) % block_out) for i0...]
    all_to_all x4, starting transfers between devices: 33.6 us -> 22.1 us  [send_each(): lax.all_to_all(shortened(pair), 'expert', split_axis=0, concat_axis=0, ti...]
    ppermute x0 -> x5, starting transfers between devices: none -> 8.09 us  [frames_begin(): lax.ppermute(val2, shard_axis, tuple(((i0, (i0 - w1) % block_out) for i0...]
  transfers between devices with their start and end apart: 9 -> 14, of which waited for: 7 -> 12; matrix products, arithmetic and copies ran while one was open for 27% -> 28% of each run, Pallas kernels for 0% -> 0%
where the time goes in v1:
time: 698 us; the launch traced here: 689 us
  waiting for transfers between devices  418 us (60%)
  local copies, waits for them, and re-layouts  158 us (23%)
  starting transfers between devices  45.3 us (6%)
  matrix products  45.1 us (6%)
  other arithmetic  19.2 us (3%)
    all_to_all x4, waiting for transfers between devices, send_each(): lax.all_to_all(shortened(pair), 'expert', split_axis=0, concat_axis=0, ti...  267 us
    all_to_all x4, waiting for transfers between devices, back_each(): lax.all_to_all(shortened(pair), 'expert', split_axis=0, concat_axis=0, ti...  137 us
    gather x2, local copies, waits for them, and re-layouts, expert_pass(): block_grads[source]  23.1 us
    all_to_all x4, starting transfers between devices, send_each(): lax.all_to_all(shortened(pair), 'expert', split_axis=0, concat_axis=0, ti...  22.1 us
    scatter x2, local copies, waits for them, and re-layouts, expert_pass(): jnp.zeros((total, width), jnp.bfloat16).at[target].set(x_flat[token_of])  21.1 us
    scatter x2, local copies, waits for them, and re-layouts, expert_pass(): jnp.zeros((total, width), jnp.bfloat16).at[target].set(grad_flat[token_of])  21 us
    scatter x2, local copies, waits for them, and re-layouts, expert_pass(): pack_grad = jnp.zeros((padded, width), jnp.bfloat16).at[place].set(got_gr...  20.1 us
    scatter x2, local copies, waits for them, and re-layouts, expert_pass(): pack_x = jnp.zeros((padded, width), jnp.bfloat16).at[place].set(got_x.res...  20.1 us
  transfers between devices with their start and end apart: 14, of which 12 were waited for; matrix products, arithmetic and copies ran while one was open for 28% of the time, Pallas kernels for 0%

profile of v1, /device:TPU:0, one launch (start us, length us, event | category | flops | bytes accessed | tf_op | source)
XLA Modules:
  0.0 688.6 jit_solution(8295650873138935281)
XLA Ops:
  28.9 10.5 %scatter_custom_fusion = bf16[1024,2048]{1,0:T(8,128)(2,1)} fusion(s32[384]{0:T(512)S(1)} %fusion.59, bf16[]{:T(256)} %constant.155.clone.1, bf16[64,2048]{1,0:T(8,128)(2,1)S(1)} %get-tuple-element.165, s32[1024]{0:T(1024)S(1)} %get-tuple-element.195), kind=kCustom, calls=%fused_computation.78 | custom fusion | bytes 4194306 | tf_op jit(solution)/shard_map/scatter | solution.py:63
  39.4 9.3 %all-to-all-start = ((bf16[32,32,2048]{2,1,0:T(8,128)(2,1)}), bf16[32,32,2048]{2,1,0:T(8,128)(2,1)}, u32[]{:S(2)}, u32[]{:S(2)}) async-start(bf16[32,32,2048]{2,1,0:T(8,128)(2,1)} %bitcast.146), calls=%async_computation | async-start | bytes 8388608 | tf_op jit(solution)/shard_map/all_to_all | solution.py:164
  48.8 10.5 %scatter_custom_fusion.2 = bf16[1024,2048]{1,0:T(8,128)(2,1)} fusion(s32[384]{0:T(512)S(1)} %fusion.59, bf16[]{:T(256)} %constant.155.clone.1, bf16[64,2048]{1,0:T(8,128)(2,1)S(1)} %get-tuple-element.163, s32[1024]{0:T(1024)S(1)} %get-tuple-element.195), kind=kCustom, calls=%fused_computation.74 | custom fusion | bytes 4194306 | tf_op jit(solution)/shard_map/scatter | solution.py:62
  59.3 83.4 %all-to-all-done = bf16[32,32,2048]{2,1,0:T(8,128)(2,1)} async-done(((bf16[32,32,2048]{2,1,0:T(8,128)(2,1)}), bf16[32,32,2048]{2,1,0:T(8,128)(2,1)}, u32[]{:S(2)}, u32[]{:S(2)}) %all-to-all-start) | async-done | bytes 4194336 | tf_op jit(solution)/shard_map/all_to_all | solution.py:164
  148.8 10.5 %scatter_custom_fusion.4 = bf16[1024,2048]{1,0:T(8,128)(2,1)} fusion(s32[384]{0:T(512)S(1)} %fusion.61, bf16[]{:T(256)} %constant.155.clone.1, bf16[64,2048]{1,0:T(8,128)(2,1)S(1)} %get-tuple-element.166, s32[1024]{0:T(1024)S(1)} %get-tuple-element.195), kind=kCustom, calls=%fused_computation.70 | custom fusion | bytes 4194306 | tf_op jit(solution)/shard_map/scatter | solution.py:63
  159.3 81.5 %all-to-all-done.1 = bf16[32,32,2048]{2,1,0:T(8,128)(2,1)} async-done(((bf16[32,32,2048]{2,1,0:T(8,128)(2,1)}), bf16[32,32,2048]{2,1,0:T(8,128)(2,1)}, u32[]{:S(2)}, u32[]{:S(2)}) %all-to-all-start.1) | async-done | bytes 4194336 | tf_op jit(solution)/shard_map/all_to_all | solution.py:164
  247.9 10.6 %scatter_custom_fusion.6 = bf16[1024,2048]{1,0:T(8,128)(2,1)} fusion(s32[384]{0:T(512)S(1)} %fusion.61, bf16[]{:T(256)} %constant.155.clone.1, bf16[64,2048]{1,0:T(8,128)(2,1)S(1)} %get-tuple-element.164, s32[1024]{0:T(1024)S(1)} %get-tuple-element.195), kind=kCustom, calls=%fused_computation.66 | custom fusion | bytes 4194306 | tf_op jit(solution)/shard_map/scatter | solution.py:62
  258.8 10.1 %scatter_custom_fusion.1 = bf16[1024,2048]{1,0:T(8,128)(2,1)} fusion(s32[1024]{0:T(1024)S(1)} %bitcast.162, bf16[1024,2048]{1,0:T(8,128)(2,1)} %bitcast.11, bf16[]{:T(256)} %constant.155.clone.1), kind=kCustom, calls=%fused_computation.76 | custom fusion | bytes 4194816 | tf_op jit(solution)/shard_map/scatter | solution.py:86
  268.8 10.0 %scatter_custom_fusion.3 = bf16[1024,2048]{1,0:T(8,128)(2,1)} fusion(s32[1024]{0:T(1024)S(1)} %bitcast.163, bf16[1024,2048]{1,0:T(8,128)(2,1)} %bitcast.15, bf16[]{:T(256)} %constant.155.clone.1), kind=kCustom, calls=%fused_computation.72 | custom fusion | bytes 4194816 | tf_op jit(solution)/shard_map/scatter | solution.py:81
  278.9 60.4 %all-to-all-done.3 = bf16[32,32,2048]{2,1,0:T(8,128)(2,1)} async-done(((bf16[32,32,2048]{2,1,0:T(8,128)(2,1)}), bf16[32,32,2048]{2,1,0:T(8,128)(2,1)}, u32[]{:S(2)}, u32[]{:S(2)}) %all-to-all-start.3) | async-done | bytes 4194336 | tf_op jit(solution)/shard_map/all_to_all | solution.py:164
  345.8 23.2 %while.25 = (s32[]{:T(128)}, bf16[1024,2048]{1,0:T(8,128)(2,1)}, bf16[1024]{0:T(1024)(128)(2,1)S(1)}, s32[]{:T(128)}, bf16[1024,2048]{1,0:T(8,128)(2,1)}, /*inde...) while((s32[]{:T(128)}, bf16[1024,2048]{1,0:T(8,128)(2,1)}, ...), condition=%wide.region_13.14_spmd, body=%wide.region_11.13_spmd.sunk | while | flops 4032102144 | bytes 69732112 | solution.py:106
  369.0 11.6 %gather_fusion = bf16[1024,2048]{1,0:T(8,128)(2,1)} fusion(bf16[1024,2048]{1,0:T(8,128)(2,1)} %get-tuple-element.100, s32[1024]{0:T(1024)S(1)} %broadcast_clamp_fusion.1), kind=kCustom, calls=%fused_computation.2 | custom fusion | bytes 8392704 | tf_op jit(solution)/shard_map/gather | solution.py:108
  380.6 10.1 %scatter_custom_fusion.5 = bf16[1024,2048]{1,0:T(8,128)(2,1)} fusion(s32[1024]{0:T(1024)S(1)} %bitcast.160, bf16[1024,2048]{1,0:T(8,128)(2,1)} %bitcast.31, bf16[]{:T(256)} %constant.155.clone.1), kind=kCustom, calls=%fused_computation.68 | custom fusion | bytes 4194816 | tf_op jit(solution)/shard_map/scatter | solution.py:86
  395.1 42.1 %all-to-all-done.4 = bf16[32,32,2048]{2,1,0:T(8,128)(2,1)} async-done(((bf16[32,32,2048]{2,1,0:T(8,128)(2,1)}), bf16[32,32,2048]{2,1,0:T(8,128)(2,1)}, u32[]{:S(2)}, u32[]{:S(2)}) %all-to-all-start.4) | async-done | bytes 4194336 | tf_op jit(solution)/shard_map/all_to_all | solution.py:164
  441.7 10.0 %scatter_custom_fusion.7 = bf16[1024,2048]{1,0:T(8,128)(2,1)} fusion(s32[1024]{0:T(1024)S(1)} %bitcast.161, bf16[1024,2048]{1,0:T(8,128)(2,1)} %bitcast.34, bf16[]{:T(256)} %constant.155.clone.1), kind=kCustom, calls=%fused_computation.64 | custom fusion | bytes 4194816 | tf_op jit(solution)/shard_map/scatter | solution.py:81
  454.2 23.1 %while.26 = (s32[]{:T(128)}, bf16[1024,2048]{1,0:T(8,128)(2,1)}, bf16[1024]{0:T(1024)(128)(2,1)S(1)}, s32[]{:T(128)}, bf16[1024,2048]{1,0:T(8,128)(2,1)}, /*inde...) while((s32[]{:T(128)}, bf16[1024,2048]{1,0:T(8,128)(2,1)}, ...), condition=%wide.region_27.28_spmd, body=%wide.region_25.27_spmd.sunk | while | flops 4032102144 | bytes 69732112 | solution.py:106
  477.3 11.6 %gather_fusion.2 = bf16[1024,2048]{1,0:T(8,128)(2,1)} fusion(bf16[1024,2048]{1,0:T(8,128)(2,1)} %get-tuple-element.101, s32[1024]{0:T(1024)S(1)} %get-tuple-element.196), kind=kCustom, calls=%fused_computation.6 | custom fusion | bytes 8392704 | tf_op jit(solution)/shard_map/gather | solution.py:108
  493.4 42.2 %all-to-all-done.2 = bf16[32,32,2048]{2,1,0:T(8,128)(2,1)} async-done(((bf16[32,32,2048]{2,1,0:T(8,128)(2,1)}), bf16[32,32,2048]{2,1,0:T(8,128)(2,1)}, u32[]{:S(2)}, u32[]{:S(2)}) %all-to-all-start.2) | async-done | bytes 4194336 | tf_op jit(solution)/shard_map/all_to_all | solution.py:171
  539.9 7.1 %gather_fusion.1 = bf16[384,2048]{1,0:T(8,128)(2,1)S(1)} fusion(bf16[1024,2048]{1,0:T(8,128)(2,1)} %bitcast.20, s32[1024]{0:T(1024)S(1)} %pad_clamp_fusion.1), kind=kCustom, calls=%fused_computation.3 | custom fusion | bytes 3147264 | tf_op jit(solution)/shard_map/gather | solution.py:116
  549.2 84.3 %all-to-all-done.5 = bf16[32,32,2048]{2,1,0:T(8,128)(2,1)} async-done(((bf16[32,32,2048]{2,1,0:T(8,128)(2,1)}), bf16[32,32,2048]{2,1,0:T(8,128)(2,1)}, u32[]{:S(2)}, u32[]{:S(2)}) %all-to-all-start.5) | async-done | bytes 4194336 | tf_op jit(solution)/shard_map/all_to_all | solution.py:171
  633.5 7.1 %gather_fusion.3 = bf16[384,2048]{1,0:T(8,128)(2,1)S(1)} fusion(bf16[1024,2048]{1,0:T(8,128)(2,1)} %bitcast.37, s32[1024]{0:T(1024)S(1)} %pad_clamp_fusion), kind=kCustom, calls=%fused_computation.7 | custom fusion | bytes 3147264 | tf_op jit(solution)/shard_map/gather | solution.py:116
  648.5 6.8 gather_fusion.4
  655.4 6.8 gather_fusion.6
  667.6 6.5 all-to-all-done.7
  (212 shorter events, 142.5 us)
Async XLA Ops:
  1.7 10.2 %collective-permute-start = (s32[1,2,32]{2,1,0:T(2,128)S(1)}, s32[1,2,32]{2,1,0:T(2,128)S(1)}, u32[]{:S(2)}, u32[]{:S(2)}) collective-permute-start(s32[1,2,32]{2,1,0:T(2,128)S(1)} %bitcast.151), channel_id=1, source_target_pairs={{0,31},{1,0},{2,1},{3,2},{4,3},{5,4},{6,5},{7,6},{8,7},{9,8},{10,9... | collective-permute-start | bytes 776 | tf_op jit(solution)/shard_map/ppermute | solution.py:134
  11.9 36.9 %copy-start.11 = (s32[384]{0:T(512)}, s32[384]{0:T(512)S(1)}, u32[]{:S(2)}) copy-start(s32[384]{0:T(512)S(1)} %fusion.59) | copy-start | bytes 4612
  11.9 3.6 collective-permute-start.1
  15.5 3.6 collective-permute-start.2
  19.2 3.7 collective-permute-start.3
  22.8 4.7 collective-permute-start.4
  22.9 222.4 %copy-start.9 = (s32[32]{0:T(128)}, s32[32]{0:T(128)S(1)}, u32[]{:S(2)}) copy-start(s32[32]{0:T(128)S(1)} %and_select_fusion.1) | copy-start | bytes 388
  27.8 217.5 %copy-start.5 = (s32[32]{0:T(128)}, s32[32]{0:T(128)S(1)}, u32[]{:S(2)}) copy-start(s32[32]{0:T(128)S(1)} %get-tuple-element.181) | copy-start | bytes 388
  27.8 217.5 %copy-start.7 = (s32[32]{0:T(128)}, s32[32]{0:T(128)S(1)}, u32[]{:S(2)}) copy-start(s32[32]{0:T(128)S(1)} %get-tuple-element.182) | copy-start | bytes 388
  39.4 103.3 %all-to-all-start = ((bf16[32,32,2048]{2,1,0:T(8,128)(2,1)}), bf16[32,32,2048]{2,1,0:T(8,128)(2,1)}, u32[]{:S(2)}, u32[]{:S(2)}) async-start(bf16[32,32,2048]{2,1,0:T(8,128)(2,1)} %bitcast.146), calls=%async_computation | async-start | bytes 8388608 | tf_op jit(solution)/shard_map/all_to_all | solution.py:164
  142.7 98.2 %all-to-all-start.1 = ((bf16[32,32,2048]{2,1,0:T(8,128)(2,1)}), bf16[32,32,2048]{2,1,0:T(8,128)(2,1)}, u32[]{:S(2)}, u32[]{:S(2)}) async-start(bf16[32,32,2048]{2,1,0:T(8,128)(2,1)} %bitcast.145), calls=%async_computation.1 | async-start | bytes 8388608 | tf_op jit(solution)/shard_map/all_to_all | solution.py:164
  240.9 98.4 %all-to-all-start.3 = ((bf16[32,32,2048]{2,1,0:T(8,128)(2,1)}), bf16[32,32,2048]{2,1,0:T(8,128)(2,1)}, u32[]{:S(2)}, u32[]{:S(2)}) async-start(bf16[32,32,2048]{2,1,0:T(8,128)(2,1)} %bitcast.143), calls=%async_computation.3 | async-start | bytes 8388608 | tf_op jit(solution)/shard_map/all_to_all | solution.py:164
  339.2 97.9 %all-to-all-start.4 = ((bf16[32,32,2048]{2,1,0:T(8,128)(2,1)}), bf16[32,32,2048]{2,1,0:T(8,128)(2,1)}, u32[]{:S(2)}, u32[]{:S(2)}) async-start(bf16[32,32,2048]{2,1,0:T(8,128)(2,1)} %bitcast.144), calls=%async_computation.4 | async-start | bytes 8388608 | tf_op jit(solution)/shard_map/all_to_all | solution.py:164
  437.2 98.4 %all-to-all-start.2 = ((bf16[32,32,2048]{2,1,0:T(8,128)(2,1)}), bf16[32,32,2048]{2,1,0:T(8,128)(2,1)}, u32[]{:S(2)}, u32[]{:S(2)}) async-start(bf16[32,32,2048]{2,1,0:T(8,128)(2,1)} %broadcast_select_fusion.1), calls=%async_computation.2 | async-start | bytes 8388608 | tf_op jit(solution)/shard_map/all_to_all | solution.py:171
  477.3 11.6 %copy-start.4 = (pred[32,32]{1,0:T(8,128)(4,1)S(1)}, pred[32,32]{1,0:T(8,128)(4,1)}, u32[]{:S(2)}) copy-start(pred[32,32]{1,0:T(8,128)(4,1)} %copy-done.3) | copy-start | bytes 3076
  493.4 46.2 %copy-start.13 = (f32[1,2,64,6]{2,1,3,0:T(2,128)S(1)}, f32[1,2,64,6]{2,1,3,0:T(2,128)}, u32[]{:S(2)}) copy-start(f32[1,2,64,6]{2,1,3,0:T(2,128)} %param.14) | copy-start | bytes 9220
  493.4 46.5 %copy-start.12 = (s32[384]{0:T(512)S(1)}, s32[384]{0:T(512)}, u32[]{:S(2)}) copy-start(s32[384]{0:T(512)} %copy-done.11) | copy-start | bytes 4612
  535.6 97.9 %all-to-all-start.5 = ((bf16[32,32,2048]{2,1,0:T(8,128)(2,1)}), bf16[32,32,2048]{2,1,0:T(8,128)(2,1)}, u32[]{:S(2)}, u32[]{:S(2)}) async-start(bf16[32,32,2048]{2,1,0:T(8,128)(2,1)} %broadcast_select_fusion), calls=%async_computation.5 | async-start | bytes 8388608 | tf_op jit(solution)/shard_map/all_to_all | solution.py:171
  648.2 14.0 %copy-start.6 = (s32[32]{0:T(128)S(1)}, s32[32]{0:T(128)}, u32[]{:S(2)}) copy-start(s32[32]{0:T(128)} %copy-done.5) | copy-start | bytes 388
  648.2 14.0 %copy-start.8 = (s32[32]{0:T(128)S(1)}, s32[32]{0:T(128)}, u32[]{:S(2)}) copy-start(s32[32]{0:T(128)} %copy-done.7) | copy-start | bytes 388
  648.3 14.0 %copy-start.10 = (s32[32]{0:T(128)S(1)}, s32[32]{0:T(128)}, u32[]{:S(2)}) copy-start(s32[32]{0:T(128)} %copy-done.9) | copy-start | bytes 388
  648.4 39.1 %collective-permute-start.5 = (bf16[1,2,64,2048]{3,2,1,0:T(8,128)(2,1)S(1)}, bf16[1,2,64,2048]{3,2,1,0:T(8,128)(2,1)S(1)}, u32[]{:S(2)}, u32[]{:S(2)}) collective-permute-start(bf16[1,2,64,2048]{3,2,1,0:T(8,128)(2,1)S(1)} %pad_maximum_fusion), channel_id=1, source_target_pairs={{0,0},{1,1},{2,2},{3,3},{4,4},{5,5},{6,6},{7,7},{8,8},{9,9},{10,10... | collective-permute-start | bytes 1572872 | tf_op jit(solution)/shard_map/ppermute | solution.py:14
  663.0 11.0 %all-to-all-start.7 = ((bf16[32,1,32]{2,1,0:T(2,128)(2,1)}), bf16[32,1,32]{2,1,0:T(2,128)(2,1)S(1)}, u32[]{:S(2)}, u32[]{:S(2)}) async-start(bf16[32,1,32]{2,1,0:T(2,128)(2,1)} %copy.105), calls=%async_computation.7 | async-start | bytes 32768 | tf_op jit(solution)/shard_map/all_to_all | solution.py:171
  674.0 9.7 %all-to-all-start.6 = ((bf16[32,1,32]{2,1,0:T(2,128)(2,1)}), bf16[32,1,32]{2,1,0:T(2,128)(2,1)S(1)}, u32[]{:S(2)}, u32[]{:S(2)}) async-start(bf16[32,1,32]{2,1,0:T(2,128)(2,1)} %copy.104), calls=%async_computation.6 | async-start | bytes 32768 | tf_op jit(solution)/shard_map/all_to_all | solution.py:171
  (16 other events, 76.2 us)
